TPU v7x, 512 devices: a whole 4x8x8 slice. The times are simulated.
512 devices in a mesh: dp: 64 (over y, z_hi, core), expert: 8 (over x, z_lo).
Axes of the slice: x: 4, y: 8, z: 8 (z_hi: 4, z_lo: 2; z = z_hi * 2 + z_lo), core: 2. Of those that a mesh axis runs over, the one named last changes fastest.
Arguments:
- activations: bfloat16 [4096, 4096], P('expert', 'dp'), may hold values from -6 to 6
- out_grad: bfloat16 [4096, 4096], P('expert', 'dp'), may hold values from -6 to 6
- w_in: bfloat16 [8, 4096, 8192], P('expert', None, 'dp'), may hold values from -0.25 to 0.25
- w_out: bfloat16 [8, 8192, 4096], P('expert', 'dp'), may hold values from -0.0625 to 0.0625
- chosen: int32 [8, 256], replicated, may hold values from 0 to 4095, as said below
- gate_scores: float32 [8, 256], P('expert'), may hold values from 0.2 to 1
Outputs:
- w_in_grad: bfloat16 [8, 4096, 8192], P('expert', None, 'dp')
- w_out_grad: bfloat16 [8, 8192, 4096], P('expert', 'dp')
- act_grad: bfloat16 [4096, 4096], P('expert', 'dp')
- gate_grad: float32 [8, 256], P('expert')
Inputs may be any that keep to these rules, and one draw needn't show every extreme that they name: Each row of chosen holds 256 distinct token numbers.
All inputs are finite; a program needn't handle non-finite values.
Results may differ from a plain program's by a relative error of at most 0.0075.
Values may be sent and summed in bfloat16 or wider, within the bound.
No kernel may reach another device: no remote copies, remote signals or barrier semaphores. Data moves between devices by JAX's collectives and lax.ppermute only.
A program may use at most 64 MiB of HBM per device.

v0:
```python
import jax
import jax.numpy as jnp
from jax import lax
from jax.sharding import PartitionSpec as P

GELU_SCALE = 0.7978845608
CUBIC_COEF = 0.044715


def gelu_parts(preact):
    inner = GELU_SCALE * (preact + CUBIC_COEF * preact * preact * preact)
    tanh_part = jnp.tanh(inner)
    gelu_val = 0.5 * preact * (1.0 + tanh_part)
    gelu_slope = 0.5 * (1.0 + tanh_part) + 0.5 * preact * (
        1.0 - tanh_part * tanh_part
    ) * GELU_SCALE * (1.0 + 3.0 * CUBIC_COEF * preact * preact)
    return (gelu_val, gelu_slope)


def contract(left_operand, right_operand, left_axis, right_axis):
    return lax.dot_general(
        left_operand,
        right_operand,
        (((left_axis,), (right_axis,)), ((), ())),
        preferred_element_type=jnp.float32,
    )


def exact_contract(left_operand, right_operand, left_axis, right_axis):
    return lax.dot_general(
        left_operand,
        right_operand,
        (((left_axis,), (right_axis,)), ((), ())),
        precision=lax.Precision.HIGHEST,
        preferred_element_type=jnp.float32,
    )


def input_sum(weight_in, preact_back):
    return lax.psum_scatter(
        contract(weight_in, preact_back, 1, 1), "dp", scatter_dimension=0, tiled=True
    )


def per_device(activations, out_grad, w_in, w_out, chosen, gate_scores):
    expert_id = lax.axis_index("expert")
    experts = lax.axis_size("expert")
    own_rows = activations.shape[0]
    every_act, every_grad = (
        lax.all_gather(activations, "expert", axis=0, tiled=True),
        lax.all_gather(out_grad, "expert", axis=0, tiled=True),
    )
    picked = lax.dynamic_index_in_dim(chosen, expert_id, 0, keepdims=False)
    inputs, upstream = (
        lax.all_gather(jnp.take(every_act, picked, axis=0), "dp", axis=1, tiled=True),
        lax.all_gather(jnp.take(every_grad, picked, axis=0), "dp", axis=1, tiled=True),
    )
    weight_in = w_in[0]
    weight_out = w_out[0]
    scores = gate_scores[0]
    gated_grad = (scores[:, None] * upstream.astype(jnp.float32)).astype(jnp.bfloat16)
    preact = jnp.dot(inputs, weight_in, preferred_element_type=jnp.float32)
    gelu_val, gelu_slope = gelu_parts(preact)
    hidden = gelu_val.astype(jnp.bfloat16)
    raw_back = contract(upstream, weight_out, 1, 1)
    gate_grad = lax.psum(jnp.sum(hidden.astype(jnp.float32) * raw_back, axis=1), "dp")
    hidden_back = contract(gated_grad, weight_out, 1, 1)
    preact_back = (hidden_back * gelu_slope).astype(jnp.bfloat16)
    weight_in_grad = contract(inputs, preact_back, 0, 0).astype(jnp.bfloat16)
    weight_out_grad = contract(hidden, gated_grad, 0, 0).astype(jnp.bfloat16)
    summed = input_sum(weight_in, preact_back)
    accumulated = jnp.zeros((summed.shape[0], own_rows), jnp.float32)
    expert_terms = lax.all_gather(summed[None], "expert", axis=0, tiled=True)
    token_ids = expert_id * own_rows + lax.iota(jnp.int32, own_rows)
    for expert_num in range(experts):
        onehot = (chosen[expert_num][None, :] == token_ids[:, None]).astype(jnp.float32)
        accumulated = accumulated + exact_contract(expert_terms[expert_num], onehot, 1, 1)
    act_grad = accumulated.T.astype(jnp.bfloat16)
    return (weight_in_grad[None], weight_out_grad[None], act_grad, gate_grad[None])


def solution(mesh):
    return jax.shard_map(
        per_device,
        mesh=mesh,
        in_specs=(
            P("expert", "dp"),
            P("expert", "dp"),
            P("expert", None, "dp"),
            P("expert", "dp", None),
            P(),
            P("expert", None),
        ),
        out_specs=(
            P("expert", None, "dp"),
            P("expert", "dp", None),
            P("expert", "dp"),
            P("expert", None),
        ),
        check_vma=False,
    )
```

profile of v0, /device:TPU:16, one launch (start us, length us, event | category | flops | bytes accessed | tf_op | source)
XLA Modules:
  0.0 458.6 jit_solution(974488165680355465)
XLA Ops:
  7.2 0.0 copy-start
  7.2 0.0 all-gather.4.cloned.1.call-start
  7.2 1.0 fusion.50
  8.3 1.0 copy.20
  9.3 1.0 copy.22
  10.2 33.9 %all_gather.17 = bf16[4096,64]{1,0:T(8,128)(2,1)S(1)} all-gather(bf16[512,64]{1,0:T(8,128)(2,1)S(1)} %copy.22), channel_id=1, replica_groups=mesh['dp'=64,'expert'=8] {'expert'}, dimensions={0}, use_global_device_ids=true | all-gather | bytes 589824 | tf_op jit(solution)/shard_map/all_gather | solution.py:51
  44.1 32.9 %all_gather.15 = bf16[4096,64]{1,0:T(8,128)(2,1)S(1)} all-gather(bf16[512,64]{1,0:T(8,128)(2,1)S(1)} %copy.20), channel_id=1, replica_groups=mesh['dp'=64,'expert'=8] {'expert'}, dimensions={0}, use_global_device_ids=true | all-gather | bytes 589824 | tf_op jit(solution)/shard_map/all_gather | solution.py:50
  77.0 0.9 gather_fusion.1
  77.9 0.0 copy-start.3
  77.9 0.9 gather_fusion
  78.8 0.1 broadcast_select_fusion
  78.9 0.0 copy-start.4
  78.9 0.7 copy.21
  79.6 0.0 all-gather.4.cloned.1.call-update
  79.6 0.0 all-gather.6.cloned.1.call-start
  79.7 0.7 copy.23
  80.4 0.0 all-gather.6.cloned.1.call-update
  80.4 0.0 reduce-scatter.4.cloned.1.call-start
  80.4 87.1 %all-gather.4.cloned.1.call-done = bf16[256,4096]{0,1:T(8,128)(2,1)} async-done(((bf16[256,64]{0,1:T(8,128)(2,1)}), bf16[256,4096]{0,1:T(8,128)(2,1)}) %all-gather.4.cloned.1.call-update) | async-done | bytes 2097168 | tf_op jit(solution)/shard_map/all_gather | solution.py:55
  167.5 0.0 copy-done
  167.5 2.3 fusion.8
  169.9 83.2 %all-gather.6.cloned.1.call-done = bf16[256,4096]{0,1:T(8,128)(2,1)} async-done(((bf16[256,64]{0,1:T(8,128)(2,1)}), bf16[256,4096]{0,1:T(8,128)(2,1)}) %all-gather.6.cloned.1.call-update) | async-done | bytes 2097168 | tf_op jit(solution)/shard_map/all_gather | solution.py:56
  253.1 0.0 copy-done.3
  253.1 0.0 copy-done.4
  253.1 2.4 fusion.4
  255.5 2.7 convolution_bitcast_fusion
  258.2 5.6 %copy.35 = f32[4096,256]{1,0:T(8,128)} copy(f32[4096,256]{0,1:T(8,128)} %convolution_bitcast_fusion) | data formatting | bytes 8388608
  263.8 0.0 reduce-scatter.4.cloned.1.call-update
  263.8 0.0 copy-start.1
  263.9 2.8 fusion.6
  266.7 121.3 %psum.7 = f32[1,256]{1,0:T(1,128)} all-reduce(f32[1,256]{1,0:T(1,128)S(1)} %bitcast.45), channel_id=1, replica_groups=mesh['dp'=64,'expert'=8] {'dp'}, use_global_device_ids=true, to_apply=%region_2.4 | all-reduce | flops 256 | bytes 2048 | tf_op jit(solution)/shard_map/psum | solution.py:66
  388.1 0.0 copy-done.1
  388.1 0.0 copy-start.2
  388.1 1.7 fusion
  389.7 0.0 copy-done.2
  389.7 1.8 fusion.1
  391.6 26.1 %reduce-scatter.4.cloned.1.call-done = f32[64,256]{1,0:T(8,128)} async-done(((f32[4096,256]{1,0:T(8,128)}), f32[64,256]{1,0:T(8,128)}) %reduce-scatter.4.cloned.1.call-update) | async-done | bytes 65552 | tf_op jit(solution)/shard_map/reduce_scatter | solution.py:40
  417.7 30.2 %all-gather = f32[512,256]{1,0:T(8,128)S(1)} all-gather(f32[64,256]{1,0:T(8,128)} %reduce-scatter.4.cloned.1.call-done), channel_id=2, replica_groups=mesh['dp'=64,'expert'=8] {'expert'}, dimensions={0}, use_global_device_ids=true | all-gather | bytes 589824 | tf_op jit(solution)/shard_map/all_gather | solution.py:73
  447.9 0.4 fusion.19
  448.3 0.4 convolution_add_fusion.6
  448.8 0.4 convolution_add_fusion.5
  449.2 0.4 convolution_add_fusion.4
  449.7 0.4 convolution_add_fusion.3
  450.1 0.4 convolution_add_fusion.2
  450.6 0.4 convolution_add_fusion.1
  451.0 1.1 fusion.5
  (4 shorter events, 0.0 us)
Async XLA Ops:
  7.2 160.4 %copy-start = (bf16[1,4096,128]{2,1,0:T(8,128)(2,1)S(1)}, bf16[1,4096,128]{2,1,0:T(8,128)(2,1)}, u32[]{:S(2)}) copy-start(bf16[1,4096,128]{2,1,0:T(8,128)(2,1)} %param.10) | copy-start | bytes 3145732
  7.2 160.3 %all-gather.4.cloned.1.call-start = ((), (), s32[]{:S(2)}) async-start(), calls=%async_computation.1 | async-start | bytes 2129920 | tf_op jit(solution)/shard_map/all_gather | solution.py:55
  77.9 175.2 %copy-start.3 = (f32[1,256]{1,0:T(1,128)S(1)}, f32[1,256]{1,0:T(1,128)}, u32[]{:S(2)}) copy-start(f32[1,256]{1,0:T(1,128)} %param.13) | copy-start | bytes 3076
  78.9 174.2 %copy-start.4 = (bf16[1,128,4096]{2,1,0:T(8,128)(2,1)S(1)}, bf16[1,128,4096]{2,1,0:T(8,128)(2,1)}, u32[]{:S(2)}) copy-start(bf16[1,128,4096]{2,1,0:T(8,128)(2,1)} %param.11) | copy-start | bytes 3145732
  79.6 173.5 %all-gather.6.cloned.1.call-start = ((), (), s32[]{:S(2)}) async-start(), calls=%async_computation.2 | async-start | bytes 2129920 | tf_op jit(solution)/shard_map/all_gather | solution.py:56
  80.4 337.3 %reduce-scatter.4.cloned.1.call-start = ((), (), s32[]{:S(2)}) async-start(), calls=%async_computation.3 | async-start | bytes 4259840 | tf_op jit(solution)/shard_map/reduce_scatter | solution.py:40
  263.8 124.2 %copy-start.1 = (bf16[256,4096]{0,1:T(8,128)(2,1)S(1)}, bf16[256,4096]{0,1:T(8,128)(2,1)}, u32[]{:S(2)}) copy-start(bf16[256,4096]{0,1:T(8,128)(2,1)} %all-gather.4.cloned.1.call-done) | copy-start | bytes 6291460
  388.1 1.7 copy-start.2
Sparse Core Ops, SparseCore 0:
  79.7 87.7 all-gather.3
  171.4 81.6 all-gather.5
  264.0 153.6 reduce-scatter.3
where the time goes:
time: 459 us
  blocking collectives  218 us (47%)
  waiting for transfers between devices  196 us (43%)
  matrix products  18 us (4%)
  between operations  13.9 us (3%)
  local copies, waits for them, and re-layouts  11.7 us (3%)
    psum x1, blocking collectives, per_device(): lax.psum(jnp.sum(hidden.astype(jnp.float32) * raw_back, axis=1), 'dp')  121 us
    all_gather x1, waiting for transfers between devices, per_device(): lax.all_gather(jnp.take(every_act, picked, axis=0), 'dp', axis=1, tiled=T...  87.1 us
    all_gather x1, waiting for transfers between devices, per_device(): lax.all_gather(jnp.take(every_grad, picked, axis=0), 'dp', axis=1, tiled=...  83.2 us
    all_gather x1, blocking collectives, per_device(): lax.all_gather(out_grad, 'expert', axis=0, tiled=True)  33.9 us
    all_gather x1, blocking collectives, per_device(): lax.all_gather(activations, 'expert', axis=0, tiled=True)  32.9 us
    all_gather x1, blocking collectives, per_device(): expert_terms = lax.all_gather(summed[None], 'expert', axis=0, tiled=True)  30.2 us
    reduce_scatter x1, waiting for transfers between devices, input_sum(): lax.psum_scatter(contract(weight_in, preact_back, 1, 1), 'dp', scatter_di...  26.1 us
    dot_general x5, matrix products, contract(): lax.dot_general(left_operand, right_operand, (((left_axis,), (right_axis,...  11.5 us
  transfers between devices with their start and end apart: 3, of which 3 were waited for; matrix products, arithmetic and copies ran while one was open for 2% of the time, Pallas kernels for 0%

commit v1 on v0

--- a/solution.py
+++ b/solution.py
@@ -70,7 +70,11 @@
     weight_out_grad = contract(hidden, gated_grad, 0, 0).astype(jnp.bfloat16)
     summed = input_sum(weight_in, preact_back)
     accumulated = jnp.zeros((summed.shape[0], own_rows), jnp.float32)
-    expert_terms = lax.all_gather(summed[None], "expert", axis=0, tiled=True)
+    own = summed[None]
+    peers = lax.axis_size("expert")
+    blocks = jnp.stack([own for _ in range(peers)])
+    blocks = lax.all_to_all(blocks, "expert", split_axis=0, concat_axis=0)
+    expert_terms = jnp.concatenate(blocks, axis=0)
     token_ids = expert_id * own_rows + lax.iota(jnp.int32, own_rows)
     for expert_num in range(experts):
         onehot = (chosen[expert_num][None, :] == token_ids[:, None]).astype(jnp.float32)

time: 459 us -> 589 us (1.28)
  the two profiles are of different devices: /device:TPU:16 before, /device:TPU:3 now
where the time goes in v1:
time: 589 us; the launch traced here: 588 us
  waiting for transfers between devices  334 us (57%)
  blocking collectives  198 us (34%)
  matrix products  24.5 us (4%)
  between operations  13.8 us (2%)
  local copies, waits for them, and re-layouts  13.4 us (2%)
    reduce_scatter x1, waiting for transfers between devices, input_sum(): lax.psum_scatter(contract(weight_in, preact_back, 1, 1), 'dp', scatter_di...  149 us
    psum x1, blocking collectives, per_device(): lax.psum(jnp.sum(hidden.astype(jnp.float32) * raw_back, axis=1), 'dp')  145 us
    all_gather x1, waiting for transfers between devices, per_device(): lax.all_gather(jnp.take(every_act, picked, axis=0), 'dp', axis=1, tiled=T...  102 us
    all_gather x1, waiting for transfers between devices, per_device(): lax.all_gather(jnp.take(every_grad, picked, axis=0), 'dp', axis=1, tiled=...  83.2 us
    all_gather x1, blocking collectives, per_device(): lax.all_gather(activations, 'expert', axis=0, tiled=True)  27.1 us
    all_gather x1, blocking collectives, per_device(): lax.all_gather(out_grad, 'expert', axis=0, tiled=True)  25.9 us
  transfers between devices with their start and end apart: 4, of which 3 were waited for; matrix products, arithmetic and copies ran while one was open for 2% of the time, Pallas kernels for 0%

profile of v1, /device:TPU:3, one launch (start us, length us, event | category | flops | bytes accessed | tf_op | source)
XLA Modules:
  0.0 588.1 jit_solution(3349319585533620086)
XLA Ops:
  7.2 0.0 copy-start
  7.2 0.0 all-gather.3.cloned.1.call-start
  7.2 1.0 fusion.42
  8.3 1.0 copy.21
  9.3 1.0 copy.23
  10.2 25.9 %all_gather.14 = bf16[4096,64]{1,0:T(8,128)(2,1)S(1)} all-gather(bf16[512,64]{1,0:T(8,128)(2,1)S(1)} %copy.23), channel_id=1, replica_groups=mesh['dp'=64,'expert'=8] {'expert'}, dimensions={0}, use_global_device_ids=true | all-gather | bytes 589824 | tf_op jit(solution)/shard_map/all_gather | solution.py:51
  36.1 27.1 %all_gather.12 = bf16[4096,64]{1,0:T(8,128)(2,1)S(1)} all-gather(bf16[512,64]{1,0:T(8,128)(2,1)S(1)} %copy.21), channel_id=1, replica_groups=mesh['dp'=64,'expert'=8] {'expert'}, dimensions={0}, use_global_device_ids=true | all-gather | bytes 589824 | tf_op jit(solution)/shard_map/all_gather | solution.py:50
  63.2 0.9 gather_fusion.1
  64.1 0.0 copy-start.3
  64.1 0.9 gather_fusion
  64.9 0.0 copy-start.4
  64.9 0.1 broadcast_select_fusion
  65.0 0.7 copy.22
  65.8 0.0 all-gather.3.cloned.1.call-update
  65.8 0.0 all-gather.5.cloned.1.call-start
  65.8 0.7 copy.24
  66.5 0.0 all-gather.5.cloned.1.call-update
  66.6 0.0 reduce-scatter.4.cloned.1.call-start
  66.6 101.6 %all-gather.3.cloned.1.call-done = bf16[256,4096]{0,1:T(8,128)(2,1)} async-done(((bf16[256,64]{0,1:T(8,128)(2,1)}), bf16[256,4096]{0,1:T(8,128)(2,1)}) %all-gather.3.cloned.1.call-update) | async-done | bytes 2097168 | tf_op jit(solution)/shard_map/all_gather | solution.py:55
  168.2 0.0 copy-done
  168.2 2.3 fusion.8
  170.5 83.2 %all-gather.5.cloned.1.call-done = bf16[256,4096]{0,1:T(8,128)(2,1)} async-done(((bf16[256,64]{0,1:T(8,128)(2,1)}), bf16[256,4096]{0,1:T(8,128)(2,1)}) %all-gather.5.cloned.1.call-update) | async-done | bytes 2097168 | tf_op jit(solution)/shard_map/all_gather | solution.py:56
  253.8 0.0 copy-done.3
  253.8 0.0 copy-done.4
  253.8 2.4 fusion.4
  256.1 2.7 convolution_bitcast_fusion
  258.8 5.6 copy.36
  264.4 0.0 reduce-scatter.4.cloned.1.call-update
  264.5 148.9 %reduce-scatter.4.cloned.1.call-done = f32[64,256]{1,0:T(8,128)} async-done(((f32[4096,256]{1,0:T(8,128)}), f32[64,256]{1,0:T(8,128)}) %reduce-scatter.4.cloned.1.call-update) | async-done | bytes 65552 | tf_op jit(solution)/shard_map/reduce_scatter | solution.py:40
  413.4 1.7 stack.3
  415.1 0.0 copy-start.1
  415.1 4.6 all-to-all-start
  419.6 2.7 fusion.6
  422.3 144.9 %psum.7 = f32[1,256]{1,0:T(1,128)} all-reduce(f32[1,256]{1,0:T(1,128)S(1)} %bitcast.69), channel_id=1, replica_groups=mesh['dp'=64,'expert'=8] {'dp'}, use_global_device_ids=true, to_apply=%region_2.4 | all-reduce | flops 256 | bytes 2048 | tf_op jit(solution)/shard_map/psum | solution.py:66
  567.2 0.0 copy-done.1
  567.2 0.0 copy-start.2
  567.2 1.7 fusion
  568.9 0.0 copy-done.2
  568.9 1.8 fusion.1
  570.7 0.0 all-to-all-done
  570.7 1.3 fusion.19
  572.0 1.3 convolution_add_fusion.6
  573.3 1.3 convolution_add_fusion.5
  574.6 1.3 convolution_add_fusion.4
  575.8 1.3 convolution_add_fusion.3
  577.1 1.3 convolution_add_fusion.2
  578.4 1.3 convolution_add_fusion.1
  579.7 1.9 fusion.5
  (4 shorter events, 0.0 us)
Async XLA Ops:
  7.2 161.0 %copy-start = (bf16[1,4096,128]{2,1,0:T(8,128)(2,1)S(1)}, bf16[1,4096,128]{2,1,0:T(8,128)(2,1)}, u32[]{:S(2)}) copy-start(bf16[1,4096,128]{2,1,0:T(8,128)(2,1)} %param.10) | copy-start | bytes 3145732
  7.2 161.0 %all-gather.3.cloned.1.call-start = ((), (), s32[]{:S(2)}) async-start(), calls=%async_computation.2 | async-start | bytes 2129920 | tf_op jit(solution)/shard_map/all_gather | solution.py:55
  64.1 189.7 %copy-start.3 = (f32[1,256]{1,0:T(1,128)S(1)}, f32[1,256]{1,0:T(1,128)}, u32[]{:S(2)}) copy-start(f32[1,256]{1,0:T(1,128)} %param.13) | copy-start | bytes 3076
  64.9 188.8 %copy-start.4 = (bf16[1,128,4096]{2,1,0:T(8,128)(2,1)S(1)}, bf16[1,128,4096]{2,1,0:T(8,128)(2,1)}, u32[]{:S(2)}) copy-start(bf16[1,128,4096]{2,1,0:T(8,128)(2,1)} %param.11) | copy-start | bytes 3145732
  65.8 188.0 %all-gather.5.cloned.1.call-start = ((), (), s32[]{:S(2)}) async-start(), calls=%async_computation.3 | async-start | bytes 2129920 | tf_op jit(solution)/shard_map/all_gather | solution.py:56
  66.6 346.8 %reduce-scatter.4.cloned.1.call-start = ((), (), s32[]{:S(2)}) async-start(), calls=%async_computation.4 | async-start | bytes 4259840 | tf_op jit(solution)/shard_map/reduce_scatter | solution.py:40
  415.1 152.1 %copy-start.1 = (bf16[256,4096]{0,1:T(8,128)(2,1)S(1)}, bf16[256,4096]{0,1:T(8,128)(2,1)}, u32[]{:S(2)}) copy-start(bf16[256,4096]{0,1:T(8,128)(2,1)} %all-gather.3.cloned.1.call-done) | copy-start | bytes 6291460
  415.1 155.6 %all-to-all-start = ((f32[8,1,64,256]{3,2,1,0:T(8,128)}), f32[8,1,64,256]{3,2,1,0:T(8,128)}, u32[]{:S(2)}, u32[]{:S(2)}) async-start(f32[8,1,64,256]{3,2,1,0:T(8,128)} %stack.3), calls=%async_computation | async-start | bytes 1048576 | tf_op jit(solution)/shard_map/all_to_all | solution.py:76
  567.2 1.7 copy-start.2
Sparse Core Ops, SparseCore 0:
  65.9 102.2 all-gather.2
  172.1 81.6 all-gather.4
  264.6 148.7 reduce-scatter.3
